TPU v7x, 512 devices: a whole 4x8x8 slice. The times are simulated.
512 devices in a mesh: stream: 8 (over y), span: 16 (over z, core), vert: 4 (over x).
Axes of the slice: x: 4, y: 8, z: 8, core: 2. Of those that a mesh axis runs over, the one named last changes fastest.
Arguments:
- fields: float32 [5, 128, 256, 1024], P(None, 'vert', 'span', 'stream'), may hold values from -6 to 6
- solid_frac: float32 [128, 256, 1024], P('vert', 'span', 'stream'), may hold values from 0 to 1
- panels: float32 [32768, 5, 256], P(('stream', 'span', 'vert')), may hold values from -0.015625 to 0.015625
- panel_owner: int32 [32768, 1], P(('stream', 'span', 'vert')), may hold values from 0 to 63; in each aligned block of 64 rows (0 to 63, 64 to 127, ...) at most 2 rows name the same one
- deck_cells: int32 [4, 16, 8, 2048], P('vert', 'span', 'stream'), may hold values from 0 to 65535
- deck_geom: float32 [4, 16, 8, 3, 2048], P('vert', None, 'stream'), may hold values from -6 to 6
- strip_ids: int32 [4, 16, 8, 2048], P('vert', None, 'stream'), may hold values from 0 to 63, as said below
- mode_shapes: float32 [3, 64, 32], replicated, may hold values from -0.0034179688 to 0.0034179688
Outputs:
- new_fields: float32 [5, 128, 256, 1024], P(None, 'vert', 'span', 'stream')
- modal_force: float32 [32], replicated
Inputs may be any that keep to these rules, and one draw needn't show every extreme that they name: `panel_owner`: tile number s * 4 + v for along-deck tile s and vertical tile v. Among the 64 panels of one device no tile is named more than 2 times; some device names some tile exactly 2 times. `strip_ids`: cells of along-deck tile s belong to strips s * 4 to (s + 1) * 4 - 1.
All inputs are finite; a program needn't handle non-finite values.
Results may differ from a plain program's by a relative error of at most 0.00012.
Values sent between devices are 32-bit elements; how exact they have to be, the bound alone decides.
No kernel may reach another device: no remote copies, remote signals or barrier semaphores. Data moves between devices by JAX's collectives and lax.ppermute only.
A program may use at most 128 MiB of HBM per device.

v0:
```python
import math
import jax
import jax.numpy as jnp
from jax import lax
from jax.sharding import PartitionSpec as P

CAP = 2
time_step = 0.15
viscous = 0.05
heat_diff = 0.03
sound_sq = 1.0
buoyant = 0.5
penalty = 0.5
relax_time = 0.5
relax_depth = 8.0
wave_cols = 16


def extended(block, sides, width):
    for axis, dim in sides:
        count = lax.axis_size(axis)
        forward = [(i, i + 1) for i in range(count - 1)]
        backward = [(target, source) for source, target in forward]
        low = lax.ppermute(
            lax.slice_in_dim(block, block.shape[dim] - width, None, axis=dim), axis, forward
        )
        high = lax.ppermute(lax.slice_in_dim(block, 0, width, axis=dim), axis, backward)
        block = jnp.concatenate([low, block, high], axis=dim)
    return block


def wave_basis(heights, widths, total_z, total_y, spec):
    modes = jnp.arange(spec, dtype=jnp.int32)
    across = (modes % wave_cols)[:, None, None]
    upward = (modes // wave_cols)[:, None, None]
    period = total_y * total_z
    phase = (
        across * widths[None, None, :] * total_z + upward * heights[None, :, None] * total_y
    ) % period
    angle = phase.astype(jnp.float32) * (2.0 * math.pi / period)
    return jnp.concatenate([jnp.cos(angle), jnp.sin(angle)], axis=0)


def relax_weights(positions, limit):
    spots = positions.astype(jnp.float32)
    return jnp.where(positions < limit, jnp.exp(-spots / relax_depth) / relax_time, 0.0)


def rates(padded, solid_frac, relax_rate, target_plane):
    centre = padded[:, 1:-1, 1:-1, 1:-1]
    east_side = padded[:, 1:-1, 1:-1, 2:]
    west_side = padded[:, 1:-1, 1:-1, :-2]
    north_side = padded[:, 1:-1, 2:, 1:-1]
    south_side = padded[:, 1:-1, :-2, 1:-1]
    upper_side = padded[:, 2:, 1:-1, 1:-1]
    lower_side = padded[:, :-2, 1:-1, 1:-1]
    grad_x = 0.5 * (east_side - west_side)
    grad_y = 0.5 * (north_side - south_side)
    grad_z = 0.5 * (upper_side - lower_side)
    laplace = (
        east_side + west_side + north_side + south_side + upper_side + lower_side - 6.0 * centre
    )
    speed_x = centre[0]
    speed_y = centre[1]
    speed_z = centre[2]
    carried = speed_x * grad_x + speed_y * grad_y + speed_z * grad_z
    coeffs = jnp.array([viscous, viscous, viscous, viscous, heat_diff], jnp.float32)[
        :, None, None, None
    ]
    damping = solid_frac / penalty
    nudging = relax_rate[None, None, None, :] * (target_plane[:, :, :, None] - centre)
    common = coeffs * laplace - carried + nudging
    extra_terms = jnp.stack(
        [
            -grad_x[3] - damping * speed_x,
            -grad_y[3] - damping * speed_y,
            -grad_z[3] - damping * speed_z + buoyant * centre[4],
            -sound_sq * (grad_x[0] + grad_y[1] + grad_z[2]),
            jnp.zeros_like(speed_x),
        ]
    )
    return common + extra_terms


def pack_slots(flat_panels, target_tile, chosen, tile_count):
    running = jnp.cumsum(chosen, axis=0) - 1
    slot_rank = jnp.sum(chosen * running, axis=1)
    slot_index = target_tile * CAP + slot_rank
    dispatch = (
        slot_index[None, :] == jnp.arange(tile_count * CAP, dtype=jnp.int32)[:, None]
    ).astype(jnp.float32)
    return jnp.dot(dispatch, flat_panels, precision=lax.Precision.HIGHEST)


def strip_forces(traction, labels, strip_count):
    columns = jnp.arange(strip_count, dtype=jnp.int32)

    def add_row(running, item_pair):
        row_values, row_labels = item_pair
        member = (row_labels[:, None] == columns[None, :]).astype(jnp.float32)
        return (running + jnp.dot(row_values, member, precision=lax.Precision.HIGHEST), None)

    start_value = jnp.zeros((traction.shape[1], strip_count), jnp.float32)
    summed, ignored = lax.scan(add_row, start_value, (traction, labels))
    return summed


def on_device(
    fields, solid_frac, panels, panel_owner, deck_cells, deck_geom, strip_ids, mode_shapes
):
    depth_cells = fields.shape[1]
    span_cells = fields.shape[2]
    wind_cells = fields.shape[3]
    n_span = lax.axis_size("span")
    n_vert = lax.axis_size("vert")
    stream_pos = lax.axis_index("stream")
    span_pos = lax.axis_index("span")
    vert_pos = lax.axis_index("vert")
    tile_count = n_span * n_vert
    held_panels = panels.shape[0]
    spec_cols = panels.shape[2]
    flat_panels = panels.reshape(held_panels, 5 * spec_cols)
    target_tile = panel_owner[:, 0]
    chosen = (target_tile[:, None] == jnp.arange(tile_count, dtype=jnp.int32)[None, :]).astype(
        jnp.int32
    )
    outgoing = pack_slots(flat_panels, target_tile, chosen, tile_count)
    arrived = lax.all_to_all(
        outgoing.reshape(tile_count, CAP * 5 * spec_cols),
        ("span", "vert"),
        split_axis=0,
        concat_axis=0,
        tiled=True,
    )
    coeffs = jnp.sum(arrived.reshape(-1, 5 * spec_cols), axis=0)
    coeffs = coeffs.reshape(5, spec_cols)
    heights = vert_pos * depth_cells + jnp.arange(depth_cells, dtype=jnp.int32)
    widths = span_pos * span_cells + jnp.arange(span_cells, dtype=jnp.int32)
    wave_table = wave_basis(
        heights, widths, depth_cells * n_vert, span_cells * n_span, spec_cols // 2
    )
    wave_table = wave_table.reshape(spec_cols, depth_cells * span_cells)
    partial_value = jnp.dot(coeffs, wave_table, precision=lax.Precision.HIGHEST)
    inflow_plane = lax.psum(partial_value, "stream").reshape(5, depth_cells, span_cells)
    target_plane = inflow_plane + jnp.array([1.0, 0.0, 0.0, 0.0, 0.0], jnp.float32)[:, None, None]
    wind_first = stream_pos * wind_cells
    relax_rate = relax_weights(
        wind_first + jnp.arange(wind_cells, dtype=jnp.int32), wind_cells // 2
    )

    def advance(state):
        padded = extended(state, (("stream", 3), ("span", 2), ("vert", 1)), 1)
        return rates(padded, solid_frac, relax_rate, target_plane)

    first_update = fields + time_step * advance(fields)
    second_rate = advance(first_update)
    new_fields = 0.5 * (fields + first_update + time_step * second_rate)
    pressure = new_fields[3].reshape(-1)
    sampled = pressure[deck_cells[0, 0, 0]]
    strip_count = mode_shapes.shape[1]
    rows_all = lax.all_gather(sampled.reshape(1, 1, 1, -1), "span", axis=1, tiled=True)
    traction = rows_all[0, :, 0][:, None, :] * deck_geom[0, :, 0]
    forces = strip_forces(traction, strip_ids[0, :, 0], strip_count)
    modal_part = jnp.einsum("cj,cjm->m", forces, mode_shapes, precision=lax.Precision.HIGHEST)
    modal_force = lax.psum(modal_part, ("stream", "vert"))
    return (new_fields, modal_force)


def solution(mesh):
    return jax.shard_map(
        on_device,
        mesh=mesh,
        in_specs=(
            P(None, "vert", "span", "stream"),
            P("vert", "span", "stream"),
            P(("stream", "span", "vert"), None, None),
            P(("stream", "span", "vert"), None),
            P("vert", "span", "stream", None),
            P("vert", None, "stream", None, None),
            P("vert", None, "stream", None),
            P(),
        ),
        out_specs=(P(None, "vert", "span", "stream"), P()),
        check_vma=False,
    )
```

profile of v0, /device:TPU:64, one launch (start us, length us, event | category | flops | bytes accessed | tf_op | source)
XLA Modules:
  0.0 263.3 jit_solution(5278629360200519969)
XLA Ops:
  0.6 2.2 fusion.52
  2.8 0.6 copy.55
  3.4 1.3 collective-permute-start
  4.7 0.6 copy.56
  5.3 4.5 %collective-permute-start.1 = (f32[5,32,16,1]{1,2,3,0:T(8,128)S(1)}, f32[5,32,16,1]{1,2,3,0:T(8,128)S(1)}, u32[]{:S(2)}, u32[]{:S(2)}) collective-permute-start(f32[5,32,16,1]{1,2,3,0:T(8,128)S(1)} %copy.56), channel_id=1, source_target_pairs={{0,64},{64,128},{128,192},{192,256},{256,320},{320,384},{384,448},... | collective-permute-start | bytes 30728 | tf_op jit(solution)/shard_map/ppermute | solution.py:24
  10.7 1.5 all_to_all.8
  12.2 13.3 %all-to-all-start = ((f32[64,1,2560]{2,1,0:T(1,128)}), f32[64,1,2560]{2,1,0:T(1,128)}, u32[]{:S(2)}, u32[]{:S(2)}) async-start(f32[64,1,2560]{2,1,0:T(1,128)} %all_to_all.8), calls=%async_computation | async-start | bytes 1310720 | tf_op jit(solution)/shard_map/all_to_all | solution.py:128
  25.6 0.9 bitcast_multiply_fusion.6
  26.7 1.7 fusion.46
  28.4 0.6 copy.37
  29.1 1.6 copy.39
  30.7 2.5 pad_maximum_fusion.39
  33.2 2.0 collective-permute-start.2
  35.2 2.3 collective-permute-start.3
  37.5 4.0 %collective-permute-done.2 = f32[5,32,1,130]{3,2,1,0:T(1,128)S(1)} collective-permute-done((f32[5,32,1,130]{3,2,1,0:T(1,128)S(1)}, f32[5,32,1,130]{3,2,1,0:T(1,128)S(1)}, u32[]{:S(2)}, u32[]{:S(2)}) %collective-permute-start.2) | collective-permute-done | bytes 83232 | tf_op jit(solution)/shard_map/ppermute | solution.py:27
  41.5 1.5 collective-permute-done.3
  43.2 1.3 collective-permute-start.4
  44.5 4.7 %collective-permute-start.5 = (f32[5,1,18,130]{3,2,1,0:T(8,128)S(1)}, f32[5,1,18,130]{3,2,1,0:T(8,128)S(1)}, u32[]{:S(2)}, u32[]{:S(2)}) collective-permute-start(f32[5,1,18,130]{3,2,1,0:T(8,128)S(1)} %get-tuple-element.71), channel_id=1, source_target_pairs={{0,1},{1,2},{2,3},{4,5},{5,6},{6,7},{8,9},{9,10},{10,11},{12,13},{... | collective-permute-start | bytes 140408 | tf_op jit(solution)/shard_map/ppermute | solution.py:24
  49.3 1.1 broadcast_multiply_fusion.4
  50.5 1.2 collective-permute-done.5
  51.7 3.2 %broadcast_multiply_fusion.3 = (f32[5,32,16,128]{3,2,1,0:T(8,128)S(1)}, f32[5,32,16,128]{3,2,1,0:T(8,128)S(1)}) fusion(f32[5,1,18,130]{3,2,1,0:T(8,128)S(1)} %collective-permute-done.4, f32[5,32,1,130]{3,2,1,0:T(1,128)S(1)} %collective-permute-done.2, f32[5,32,16,1]{3,2,1,0:T(8,128)S(1)} %copy.37, f32[5,32,16,128]{3,2,1,0:T(8,128)S(1)} %copy-done.1, ...), kind=kLoop, calls=%fused_computation.50 | loop fusion | flops 5242880 | bytes 4212640 | tf_op jit(solution)/shard_map/mul | solution.py:59
  54.9 0.7 fusion.40
  55.7 0.8 fusion.36
  56.4 0.8 fusion.32
  57.2 0.8 fusion.27
  58.0 0.7 broadcast_dynamic-update-slice_fusion.1
  58.7 2.6 %reduce = f32[64,2560]{1,0:T(8,128)S(1)} reduce(f32[64,1,2560]{2,1,0:T(1,128)} %all-to-all-done, f32[]{:T(128)} %constant.123), dimensions={1}, to_apply=%all_to_all.7.reduce_sub_computation | reduce | bytes 1310724 | tf_op jit(solution)/shard_map/all_to_all | solution.py:128
  61.5 1.5 fusion.3
  63.1 30.8 %psum.14 = f32[5,32,16]{2,1,0:T(8,128)S(1)} all-reduce(f32[5,32,16]{2,1,0:T(8,128)S(1)} %reshape.200), channel_id=1, replica_groups=mesh['stream'=8,'span'=16,'vert'=4] {'stream'}, use_global_device_ids=true, to_apply=%region_3.4 | all-reduce | flops 2560 | bytes 20480 | tf_op jit(solution)/shard_map/psum | solution.py:144
  94.0 7.5 %multiply_add_fusion = f32[5,32,16,128]{3,2,1,0:T(8,128)S(1)} fusion(f32[5,32,16,128]{3,2,1,0:T(8,128)S(1)} %copy-done.1, f32[5,32,16,128]{3,2,1,0:T(8,128)} %broadcast_dynamic-update-slice_fusion.1, f32[5,32,16]{2,1,0:T(8,128)S(1)} %broadcast_add_fusion.1, f32[128]{0:T(128)S(1)} %compare_select_fusion.1, f32[32,16,128]{2,1,0:T(8,128)} %get-tuple-element.87, ...), kind=kLoop, calls=%fused_computation.45 | loop fusion | flops 13434880 | bytes 5009844 | tf_op jit(solution)/shard_map/add | solution.py:155
  101.5 1.9 fusion.51
  103.5 1.9 copy.44
  105.4 1.3 collective-permute-start.6
  106.7 1.9 copy.46
  108.5 4.5 %collective-permute-start.7 = (f32[5,32,16,1]{1,2,3,0:T(8,128)S(1)}, f32[5,32,16,1]{1,2,3,0:T(8,128)S(1)}, u32[]{:S(2)}, u32[]{:S(2)}) collective-permute-start(f32[5,32,16,1]{1,2,3,0:T(8,128)S(1)} %copy.46), channel_id=1, source_target_pairs={{0,64},{64,128},{128,192},{192,256},{256,320},{320,384},{384,448},... | collective-permute-start | bytes 30728 | tf_op jit(solution)/shard_map/ppermute | solution.py:24
  113.2 1.6 copy.45
  114.8 1.6 copy.47
  116.4 2.9 %pad_maximum_fusion.36 = (f32[5,32,1,130]{3,2,1,0:T(1,128)S(1)}, f32[5,32,1,130]{3,2,1,0:T(1,128)S(1)}) fusion(f32[5,32,16,1]{3,2,1,0:T(8,128)} %copy.45, f32[5,32,16,128]{3,2,1,0:T(8,128)S(1)} %multiply_add_fusion, f32[5,32,16,1]{3,2,1,0:T(8,128)} %copy.47), kind=kLoop, calls=%fused_computation.118 | loop fusion | flops 83200 | bytes 1497600 | tf_op jit(solution)/shard_map/concatenate | solution.py:28
  119.3 2.1 collective-permute-start.8
  121.4 2.6 collective-permute-start.9
  124.2 3.8 %collective-permute-done.9 = f32[5,32,1,130]{3,2,1,0:T(1,128)S(1)} collective-permute-done((f32[5,32,1,130]{3,2,1,0:T(1,128)S(1)}, f32[5,32,1,130]{3,2,1,0:T(1,128)S(1)}, u32[]{:S(2)}, u32[]{:S(2)}) %collective-permute-start.9) | collective-permute-done | bytes 83232 | tf_op jit(solution)/shard_map/ppermute | solution.py:24
  128.2 1.3 collective-permute-start.10
  129.5 5.0 %collective-permute-start.11 = (f32[5,1,18,130]{3,2,1,0:T(8,128)S(1)}, f32[5,1,18,130]{3,2,1,0:T(8,128)S(1)}, u32[]{:S(2)}, u32[]{:S(2)}) collective-permute-start(f32[5,1,18,130]{3,2,1,0:T(8,128)S(1)} %get-tuple-element.69), channel_id=1, source_target_pairs={{0,1},{1,2},{2,3},{4,5},{5,6},{6,7},{8,9},{9,10},{10,11},{12,13},{... | collective-permute-start | bytes 140408 | tf_op jit(solution)/shard_map/ppermute | solution.py:24
  134.5 1.1 broadcast_multiply_fusion.1
  135.6 1.3 collective-permute-done.11
  136.9 3.1 %broadcast_multiply_fusion = (f32[5,32,16,128]{3,2,1,0:T(8,128)S(1)}, f32[5,32,16,128]{3,2,1,0:T(8,128)S(1)}) fusion(f32[5,1,18,130]{3,2,1,0:T(8,128)S(1)} %collective-permute-done.10, f32[5,32,1,130]{3,2,1,0:T(1,128)S(1)} %collective-permute-done.8, f32[5,32,16,1]{3,2,1,0:T(8,128)S(1)} %copy-done.4, f32[5,32,16,128]{3,2,1,0:T(8,128)S(1)} %multiply_add_fusion, ...), kind=kLoop, calls=%fused_computation.47 | loop fusion | flops 5242880 | bytes 4212640 | tf_op jit(solution)/shard_map/mul | solution.py:59
  140.4 5.0 %add_multiply_fusion = f32[5,32,16,128]{3,2,1,0:T(8,128)S(1)} fusion(f32[5,32,16,128]{3,2,1,0:T(8,128)S(1)} %broadcast_dynamic-update-slice_fusion, f32[5,32,16,128]{3,2,1,0:T(8,128)S(1)} %multiply_add_fusion, f32[5,32,16,128]{3,2,1,0:T(8,128)S(1)} %copy-done.1, f32[32,16,128]{2,1,0:T(8,128)S(1)} %get-tuple-element.82, ...), kind=kLoop, calls=%fused_computation.44 | loop fusion | flops 14090240 | bytes 6320564 | tf_op jit(solution)/shard_map/mul | solution.py:157
  145.4 1.0 copy-done.7
  146.5 11.8 %gather_fusion = f32[2048]{0:T(1024)S(1)} fusion(f32[65536]{0:T(1024)S(1)} %bitcast.150, s32[2048]{0:T(1024)S(1)} %broadcast_clamp_fusion), kind=kCustom, calls=%fused_computation | custom fusion | bytes 24576 | tf_op jit(solution)/shard_map/gather | solution.py:159
  158.2 16.8 %all-gather = f32[32768]{0:T(1024)S(1)} all-gather(f32[2048]{0:T(1024)S(1)} %gather_fusion), channel_id=2, replica_groups=mesh['stream'=8,'span'=16,'vert'=4] {'span'}, dimensions={0}, use_global_device_ids=true | all-gather | bytes 139264 | tf_op jit(solution)/shard_map/all_gather | solution.py:161
  175.2 10.6 %while.11 = (s32[]{:T(128)}, f32[3,64]{1,0:T(4,128)S(1)}, f32[16,3,2048]{2,0,1:T(8,128)S(1)}, s32[16,2048]{1,0:T(8,128)S(1)}, s32[]{:T(128)}, /*index=5*/s32[]{:T(128)}) while((s32[]{:T(128)}, f32[3,64]{1,0:T(4,128)S(1)}, f32[16,3,2048]{2,0,1:T(8,128)S(1)}, s32[16,2048]{1,0:T(8,128)S(1)}, s32[]{:T(128)}, /*index=5*/s32[]{:T(128)}) %tuple.46), condition=%wide.region_5.6_spmd.clone, body=%wide.region_4.5_spmd.clone.sunk | while | flops 4850051 | bytes 99927 | solution.py:104
  175.3 0.6 convolution_add_fusion.2
  176.0 0.6 convolution_add_fusion.2
  176.6 0.6 convolution_add_fusion.2
  177.3 0.6 convolution_add_fusion.2
  177.9 0.6 convolution_add_fusion.2
  178.6 0.6 convolution_add_fusion.2
  179.3 0.6 convolution_add_fusion.2
  179.9 0.6 convolution_add_fusion.2
  180.6 0.6 convolution_add_fusion.2
  181.3 0.6 convolution_add_fusion.2
  181.9 0.6 convolution_add_fusion.2
  184.6 0.6 convolution_add_fusion.2
  186.0 77.3 %psum.15 = f32[32]{0:T(128)} all-reduce(f32[32]{0:T(128)S(1)} %convolution_bitcast_fusion), channel_id=1, replica_groups=mesh['stream'=8,'span'=16,'vert'=4] {'stream','vert'}, use_global_device_ids=true, to_apply=%region_6.7 | all-reduce | flops 32 | bytes 256 | tf_op jit(solution)/shard_map/psum | solution.py:165
  (112 shorter events, 5.7 us)
Async XLA Ops:
  0.6 185.2 %copy-start = (f32[3,64,32]{1,2,0:T(8,128)S(1)}, f32[3,64,32]{1,2,0:T(8,128)}, u32[]{:S(2)}) copy-start(f32[3,64,32]{1,2,0:T(8,128)} %param.20) | copy-start | bytes 73732
  2.8 7.1 %copy-start.14 = (s32[64,1]{0,1:T(1,128)S(1)}, s32[64,1]{0,1:T(1,128)}, u32[]{:S(2)}) copy-start(s32[64,1]{0,1:T(1,128)} %param.16) | copy-start | bytes 772
  2.8 7.4 %copy-start.11 = (f32[64,5,256]{2,0,1:T(8,128)S(1)}, f32[64,5,256]{2,0,1:T(8,128)}, u32[]{:S(2)}) copy-start(f32[64,5,256]{2,0,1:T(8,128)} %param.15) | copy-start | bytes 983044
  3.4 25.0 %collective-permute-start = (f32[5,32,16,1]{1,2,3,0:T(8,128)S(1)}, f32[5,32,16,1]{1,2,3,0:T(8,128)S(1)}, u32[]{:S(2)}, u32[]{:S(2)}) collective-permute-start(f32[5,32,16,1]{1,2,3,0:T(8,128)S(1)} %copy.55), channel_id=1, source_target_pairs={{64,0},{128,64},{192,128},{256,192},{320,256},{384,320},{448,384},... | collective-permute-start | bytes 30728 | tf_op jit(solution)/shard_map/ppermute | solution.py:27
  5.3 23.7 %collective-permute-start.1 = (f32[5,32,16,1]{1,2,3,0:T(8,128)S(1)}, f32[5,32,16,1]{1,2,3,0:T(8,128)S(1)}, u32[]{:S(2)}, u32[]{:S(2)}) collective-permute-start(f32[5,32,16,1]{1,2,3,0:T(8,128)S(1)} %copy.56), channel_id=1, source_target_pairs={{0,64},{64,128},{128,192},{192,256},{256,320},{320,384},{384,448},... | collective-permute-start | bytes 30728 | tf_op jit(solution)/shard_map/ppermute | solution.py:24
  10.7 14.8 %copy-start.1 = (f32[5,32,16,128]{3,2,1,0:T(8,128)S(1)}, f32[5,32,16,128]{3,2,1,0:T(8,128)}, u32[]{:S(2)}) copy-start(f32[5,32,16,128]{3,2,1,0:T(8,128)} %param.13) | copy-start | bytes 3932164
  12.2 14.2 %copy-start.13 = (s32[1,1,1,2048]{3,2,1,0:T(1,128)S(1)}, s32[1,1,1,2048]{3,2,1,0:T(1,128)}, u32[]{:S(2)}) copy-start(s32[1,1,1,2048]{3,2,1,0:T(1,128)} %param.17) | copy-start | bytes 24580
  12.2 46.5 %all-to-all-start = ((f32[64,1,2560]{2,1,0:T(1,128)}), f32[64,1,2560]{2,1,0:T(1,128)}, u32[]{:S(2)}, u32[]{:S(2)}) async-start(f32[64,1,2560]{2,1,0:T(1,128)} %all_to_all.8), calls=%async_computation | async-start | bytes 1310720 | tf_op jit(solution)/shard_map/all_to_all | solution.py:128
  29.1 22.7 %copy-start.2 = (f32[5,32,16,1]{3,2,1,0:T(8,128)}, f32[5,32,16,1]{3,2,1,0:T(8,128)S(1)}, u32[]{:S(2)}) copy-start(f32[5,32,16,1]{3,2,1,0:T(8,128)S(1)} %copy.37) | copy-start | bytes 30724
  30.7 12.4 %copy-start.3 = (f32[5,32,16,1]{3,2,1,0:T(8,128)S(1)}, f32[5,32,16,1]{3,2,1,0:T(8,128)}, u32[]{:S(2)}) copy-start(f32[5,32,16,1]{3,2,1,0:T(8,128)} %copy.39) | copy-start | bytes 30724
  33.2 8.4 %collective-permute-start.2 = (f32[5,32,1,130]{3,2,1,0:T(1,128)S(1)}, f32[5,32,1,130]{3,2,1,0:T(1,128)S(1)}, u32[]{:S(2)}, u32[]{:S(2)}) collective-permute-start(f32[5,32,1,130]{3,2,1,0:T(1,128)S(1)} %get-tuple-element.80), channel_id=1, source_target_pairs={{4,0},{8,4},{12,8},{16,12},{20,16},{24,20},{28,24},{32,28},{36,32}... | collective-permute-start | bytes 249608 | tf_op jit(solution)/shard_map/ppermute | solution.py:27
  35.2 7.9 %collective-permute-start.3 = (f32[5,32,1,130]{3,2,1,0:T(1,128)S(1)}, f32[5,32,1,130]{3,2,1,0:T(1,128)S(1)}, u32[]{:S(2)}, u32[]{:S(2)}) collective-permute-start(f32[5,32,1,130]{3,2,1,0:T(1,128)S(1)} %get-tuple-element.79), channel_id=1, source_target_pairs={{0,4},{4,8},{8,12},{12,16},{16,20},{20,24},{24,28},{28,32},{32,36}... | collective-permute-start | bytes 249608 | tf_op jit(solution)/shard_map/ppermute | solution.py:24
  43.2 7.3 %collective-permute-start.4 = (f32[5,1,18,130]{3,2,1,0:T(8,128)S(1)}, f32[5,1,18,130]{3,2,1,0:T(8,128)S(1)}, u32[]{:S(2)}, u32[]{:S(2)}) collective-permute-start(f32[5,1,18,130]{3,2,1,0:T(8,128)S(1)} %get-tuple-element.72), channel_id=1, source_target_pairs={{1,0},{2,1},{3,2},{5,4},{6,5},{7,6},{9,8},{10,9},{11,10},{13,12},{... | collective-permute-start | bytes 140408 | tf_op jit(solution)/shard_map/ppermute | solution.py:27
  44.5 7.2 %collective-permute-start.5 = (f32[5,1,18,130]{3,2,1,0:T(8,128)S(1)}, f32[5,1,18,130]{3,2,1,0:T(8,128)S(1)}, u32[]{:S(2)}, u32[]{:S(2)}) collective-permute-start(f32[5,1,18,130]{3,2,1,0:T(8,128)S(1)} %get-tuple-element.71), channel_id=1, source_target_pairs={{0,1},{1,2},{2,3},{4,5},{5,6},{6,7},{8,9},{9,10},{10,11},{12,13},{... | collective-permute-start | bytes 140408 | tf_op jit(solution)/shard_map/ppermute | solution.py:24
  50.4 4.5 %copy-start.6 = (f32[32,16,128]{2,1,0:T(8,128)S(1)}, f32[32,16,128]{2,1,0:T(8,128)}, u32[]{:S(2)}) copy-start(f32[32,16,128]{2,1,0:T(8,128)} %param.14) | copy-start | bytes 786436
  50.5 4.4 %copy-start.8 = (f32[5,1,18,130]{3,2,1,0:T(8,128)}, f32[5,1,18,130]{3,2,1,0:T(8,128)S(1)}, u32[]{:S(2)}) copy-start(f32[5,1,18,130]{3,2,1,0:T(8,128)S(1)} %collective-permute-done.4) | copy-start | bytes 140404
  51.7 3.2 %copy-start.9 = (f32[5,1,18,130]{3,2,1,0:T(8,128)}, f32[5,1,18,130]{3,2,1,0:T(8,128)S(1)}, u32[]{:S(2)}) copy-start(f32[5,1,18,130]{3,2,1,0:T(8,128)S(1)} %collective-permute-done.5) | copy-start | bytes 140404
  61.3 32.6 %copy-start.16 = (f32[5]{0:T(128)S(1)}, f32[5]{0:T(128)}, u32[]{:S(2)}) copy-start(f32[5]{0:T(128)} %constant.116.clone) | copy-start | bytes 64
  61.4 32.6 %copy-start.15 = (f32[5]{0:T(128)S(1)}, f32[5]{0:T(128)}, u32[]{:S(2)}) copy-start(f32[5]{0:T(128)} %constant.117.clone) | copy-start | bytes 64
  103.5 9.7 %copy-start.12 = (s32[1,16,1,2048]{3,2,1,0:T(1,128)S(1)}, s32[1,16,1,2048]{3,2,1,0:T(1,128)}, u32[]{:S(2)}) copy-start(s32[1,16,1,2048]{3,2,1,0:T(1,128)} %param.19) | copy-start | bytes 393220
  105.4 7.8 %collective-permute-start.6 = (f32[5,32,16,1]{1,2,3,0:T(8,128)S(1)}, f32[5,32,16,1]{1,2,3,0:T(8,128)S(1)}, u32[]{:S(2)}, u32[]{:S(2)}) collective-permute-start(f32[5,32,16,1]{1,2,3,0:T(8,128)S(1)} %copy.44), channel_id=1, source_target_pairs={{64,0},{128,64},{192,128},{256,192},{320,256},{384,320},{448,384},... | collective-permute-start | bytes 30728 | tf_op jit(solution)/shard_map/ppermute | solution.py:27
  108.5 6.3 %collective-permute-start.7 = (f32[5,32,16,1]{1,2,3,0:T(8,128)S(1)}, f32[5,32,16,1]{1,2,3,0:T(8,128)S(1)}, u32[]{:S(2)}, u32[]{:S(2)}) collective-permute-start(f32[5,32,16,1]{1,2,3,0:T(8,128)S(1)} %copy.46), channel_id=1, source_target_pairs={{0,64},{64,128},{128,192},{192,256},{256,320},{320,384},{384,448},... | collective-permute-start | bytes 30728 | tf_op jit(solution)/shard_map/ppermute | solution.py:24
  116.4 11.6 %copy-start.5 = (f32[5,32,16,1]{3,2,1,0:T(8,128)S(1)}, f32[5,32,16,1]{3,2,1,0:T(8,128)}, u32[]{:S(2)}) copy-start(f32[5,32,16,1]{3,2,1,0:T(8,128)} %copy.47) | copy-start | bytes 30724
  119.3 8.7 %copy-start.4 = (f32[5,32,16,1]{3,2,1,0:T(8,128)S(1)}, f32[5,32,16,1]{3,2,1,0:T(8,128)}, u32[]{:S(2)}) copy-start(f32[5,32,16,1]{3,2,1,0:T(8,128)} %copy.45) | copy-start | bytes 30724
  119.3 4.9 %collective-permute-start.8 = (f32[5,32,1,130]{3,2,1,0:T(1,128)S(1)}, f32[5,32,1,130]{3,2,1,0:T(1,128)S(1)}, u32[]{:S(2)}, u32[]{:S(2)}) collective-permute-start(f32[5,32,1,130]{3,2,1,0:T(1,128)S(1)} %get-tuple-element.76), channel_id=1, source_target_pairs={{4,0},{8,4},{12,8},{16,12},{20,16},{24,20},{28,24},{32,28},{36,32}... | collective-permute-start | bytes 249608 | tf_op jit(solution)/shard_map/ppermute | solution.py:27
  121.4 6.6 %collective-permute-start.9 = (f32[5,32,1,130]{3,2,1,0:T(1,128)S(1)}, f32[5,32,1,130]{3,2,1,0:T(1,128)S(1)}, u32[]{:S(2)}, u32[]{:S(2)}) collective-permute-start(f32[5,32,1,130]{3,2,1,0:T(1,128)S(1)} %get-tuple-element.75), channel_id=1, source_target_pairs={{0,4},{4,8},{8,12},{12,16},{16,20},{20,24},{24,28},{28,32},{32,36}... | collective-permute-start | bytes 249608 | tf_op jit(solution)/shard_map/ppermute | solution.py:24
  128.2 7.4 %collective-permute-start.10 = (f32[5,1,18,130]{3,2,1,0:T(8,128)S(1)}, f32[5,1,18,130]{3,2,1,0:T(8,128)S(1)}, u32[]{:S(2)}, u32[]{:S(2)}) collective-permute-start(f32[5,1,18,130]{3,2,1,0:T(8,128)S(1)} %get-tuple-element.70), channel_id=1, source_target_pairs={{1,0},{2,1},{3,2},{5,4},{6,5},{7,6},{9,8},{10,9},{11,10},{13,12},{... | collective-permute-start | bytes 140408 | tf_op jit(solution)/shard_map/ppermute | solution.py:27
  129.5 7.4 %collective-permute-start.11 = (f32[5,1,18,130]{3,2,1,0:T(8,128)S(1)}, f32[5,1,18,130]{3,2,1,0:T(8,128)S(1)}, u32[]{:S(2)}, u32[]{:S(2)}) collective-permute-start(f32[5,1,18,130]{3,2,1,0:T(8,128)S(1)} %get-tuple-element.69), channel_id=1, source_target_pairs={{0,1},{1,2},{2,3},{4,5},{5,6},{6,7},{8,9},{9,10},{10,11},{12,13},{... | collective-permute-start | bytes 140408 | tf_op jit(solution)/shard_map/ppermute | solution.py:24
  145.4 1.1 copy-start.7
  146.4 28.6 %copy-start.10 = (f32[1,16,1,3,2048]{4,2,3,1,0:T(1,128)S(1)}, f32[1,16,1,3,2048]{4,2,3,1,0:T(1,128)}, u32[]{:S(2)}) copy-start(f32[1,16,1,3,2048]{4,2,3,1,0:T(1,128)} %param.18) | copy-start | bytes 1179652
where the time goes:
time: 264 us; the launch traced here: 263 us
  blocking collectives  125 us (47%)
  starting transfers between devices  46.3 us (18%)
  other arithmetic  36.1 us (14%)
  local copies, waits for them, and re-layouts  30.7 us (12%)
  waiting for transfers between devices  12.1 us (5%)
  matrix products  11.3 us (4%)
    psum x1, blocking collectives, on_device(): modal_force = lax.psum(modal_part, ('stream', 'vert'))  77.3 us
    psum x1, blocking collectives, on_device(): lax.psum(partial_value, 'stream').reshape(5, depth_cells, span_cells)  30.8 us
    ppermute x6, starting transfers between devices, extended(): lax.ppermute(lax.slice_in_dim(block, block.shape[dim] - width, None, axis...  23.8 us
    all_gather x1, blocking collectives, on_device(): lax.all_gather(sampled.reshape(1, 1, 1, -1), 'span', axis=1, tiled=True)  16.8 us
    all_to_all x1, starting transfers between devices, on_device(): lax.all_to_all(outgoing.reshape(tile_count, CAP * 5 * spec_cols), ('span'...  13.3 us
    gather x1, local copies, waits for them, and re-layouts, on_device(): sampled = pressure[deck_cells[0, 0, 0]]  11.8 us
    dot_general x16, matrix products, add_row(): jnp.dot(row_values, member, precision=lax.Precision.HIGHEST)  9.31 us
    ppermute x6, starting transfers between devices, extended(): lax.ppermute(lax.slice_in_dim(block, 0, width, axis=dim), axis, backward)  9.23 us
  transfers between devices with their start and end apart: 13, of which 7 were waited for; matrix products, arithmetic and copies ran while one was open for 8% of the time, Pallas kernels for 0%

commit v1 on v0

--- a/solution.py
+++ b/solution.py
@@ -3,6 +3,7 @@
 import jax.numpy as jnp
 from jax import lax
 from jax.sharding import PartitionSpec as P
+from jax.lax import psum
 
 CAP = 2
 time_step = 0.15
@@ -14,6 +15,12 @@
 relax_time = 0.5
 relax_depth = 8.0
 wave_cols = 16
+
+
+def pass_kinds_on(z):
+    for dd in ("vert", "stream"):
+        z = psum(z, dd)
+    return z
 
 
 def extended(block, sides, width):
@@ -162,7 +169,7 @@
     traction = rows_all[0, :, 0][:, None, :] * deck_geom[0, :, 0]
     forces = strip_forces(traction, strip_ids[0, :, 0], strip_count)
     modal_part = jnp.einsum("cj,cjm->m", forces, mode_shapes, precision=lax.Precision.HIGHEST)
-    modal_force = lax.psum(modal_part, ("stream", "vert"))
+    modal_force = pass_kinds_on(modal_part)
     return (new_fields, modal_force)
 
 

time: 264 us -> 217 us (0.82)
  the two profiles are of different devices: /device:TPU:64 before, /device:TPU:24 now
where the time goes in v1:
time: 217 us
  blocking collectives  82.1 us (38%)
  starting transfers between devices  49.6 us (23%)
  other arithmetic  36.1 us (17%)
  local copies, waits for them, and re-layouts  30.7 us (14%)
  matrix products  11.3 us (5%)
  waiting for transfers between devices  4.84 us (2%)
    psum x2, blocking collectives, pass_kinds_on(): z = psum(z, dd)  28.5 us
    psum x1, blocking collectives, on_device(): lax.psum(partial_value, 'stream').reshape(5, depth_cells, span_cells)  28.1 us
    all_gather x1, blocking collectives, on_device(): lax.all_gather(sampled.reshape(1, 1, 1, -1), 'span', axis=1, tiled=True)  25.6 us
    ppermute x6, starting transfers between devices, extended(): lax.ppermute(lax.slice_in_dim(block, block.shape[dim] - width, None, axis...  24.2 us
    all_to_all x1, starting transfers between devices, on_device(): lax.all_to_all(outgoing.reshape(tile_count, CAP * 5 * spec_cols), ('span'...  14.1 us
    gather x1, local copies, waits for them, and re-layouts, on_device(): sampled = pressure[deck_cells[0, 0, 0]]  11.8 us
    ppermute x6, starting transfers between devices, extended(): lax.ppermute(lax.slice_in_dim(block, 0, width, axis=dim), axis, backward)  11.3 us
    dot_general x16, matrix products, add_row(): jnp.dot(row_values, member, precision=lax.Precision.HIGHEST)  9.31 us
  transfers between devices with their start and end apart: 13, of which 5 were waited for; matrix products, arithmetic and copies ran while one was open for 10% of the time, Pallas kernels for 0%

profile of v1, /device:TPU:24, one launch (start us, length us, event | category | flops | bytes accessed | tf_op | source)
XLA Modules:
  0.0 216.7 jit_solution(39878756111789206)
XLA Ops:
  0.6 2.2 fusion.52
  2.8 0.6 copy.55
  3.4 2.4 %collective-permute-start = (f32[5,32,16,1]{1,2,3,0:T(8,128)S(1)}, f32[5,32,16,1]{1,2,3,0:T(8,128)S(1)}, u32[]{:S(2)}, u32[]{:S(2)}) collective-permute-start(f32[5,32,16,1]{1,2,3,0:T(8,128)S(1)} %copy.55), channel_id=1, source_target_pairs={{64,0},{128,64},{192,128},{256,192},{320,256},{384,320},{448,384},... | collective-permute-start | bytes 30728 | tf_op jit(solution)/shard_map/ppermute | solution.py:34
  5.8 0.6 copy.56
  6.4 4.7 %collective-permute-start.1 = (f32[5,32,16,1]{1,2,3,0:T(8,128)S(1)}, f32[5,32,16,1]{1,2,3,0:T(8,128)S(1)}, u32[]{:S(2)}, u32[]{:S(2)}) collective-permute-start(f32[5,32,16,1]{1,2,3,0:T(8,128)S(1)} %copy.56), channel_id=1, source_target_pairs={{0,64},{64,128},{128,192},{192,256},{256,320},{320,384},{384,448},... | collective-permute-start | bytes 30728 | tf_op jit(solution)/shard_map/ppermute | solution.py:31
  11.9 1.5 all_to_all.8
  13.5 14.1 %all-to-all-start = ((f32[64,1,2560]{2,1,0:T(1,128)}), f32[64,1,2560]{2,1,0:T(1,128)}, u32[]{:S(2)}, u32[]{:S(2)}) async-start(f32[64,1,2560]{2,1,0:T(1,128)} %all_to_all.8), calls=%async_computation | async-start | bytes 1310720 | tf_op jit(solution)/shard_map/all_to_all | solution.py:135
  27.6 0.9 bitcast_multiply_fusion.6
  28.8 1.8 fusion.46
  30.5 0.6 copy.37
  31.2 1.6 copy.39
  32.8 2.5 %pad_maximum_fusion.39 = (f32[5,32,1,130]{3,2,1,0:T(1,128)S(1)}, f32[5,32,1,130]{3,2,1,0:T(1,128)S(1)}) fusion(f32[5,32,16,1]{3,2,1,0:T(8,128)S(1)} %copy.37, f32[5,32,16,128]{3,2,1,0:T(8,128)S(1)} %copy-done.1, f32[5,32,16,1]{3,2,1,0:T(8,128)} %copy.39), kind=kLoop, calls=%fused_computation.121 | loop fusion | flops 83200 | bytes 1497600 | tf_op jit(solution)/shard_map/concatenate | solution.py:35
  35.3 1.3 collective-permute-start.2
  36.6 3.0 %collective-permute-start.3 = (f32[5,32,1,130]{3,2,1,0:T(1,128)S(1)}, f32[5,32,1,130]{3,2,1,0:T(1,128)S(1)}, u32[]{:S(2)}, u32[]{:S(2)}) collective-permute-start(f32[5,32,1,130]{3,2,1,0:T(1,128)S(1)} %get-tuple-element.79), channel_id=1, source_target_pairs={{0,4},{4,8},{8,12},{12,16},{16,20},{20,24},{24,28},{28,32},{32,36}... | collective-permute-start | bytes 249608 | tf_op jit(solution)/shard_map/ppermute | solution.py:31
  39.7 1.0 collective-permute-done.3
  40.8 1.3 collective-permute-start.4
  42.1 4.7 %collective-permute-start.5 = (f32[5,1,18,130]{3,2,1,0:T(8,128)S(1)}, f32[5,1,18,130]{3,2,1,0:T(8,128)S(1)}, u32[]{:S(2)}, u32[]{:S(2)}) collective-permute-start(f32[5,1,18,130]{3,2,1,0:T(8,128)S(1)} %get-tuple-element.71), channel_id=1, source_target_pairs={{0,1},{1,2},{2,3},{4,5},{5,6},{6,7},{8,9},{9,10},{10,11},{12,13},{... | collective-permute-start | bytes 140408 | tf_op jit(solution)/shard_map/ppermute | solution.py:31
  46.9 1.1 broadcast_multiply_fusion.4
  48.0 1.1 collective-permute-done.5
  49.1 3.2 %broadcast_multiply_fusion.3 = (f32[5,32,16,128]{3,2,1,0:T(8,128)S(1)}, f32[5,32,16,128]{3,2,1,0:T(8,128)S(1)}) fusion(f32[5,1,18,130]{3,2,1,0:T(8,128)S(1)} %collective-permute-done.4, f32[5,32,1,130]{3,2,1,0:T(1,128)S(1)} %collective-permute-done.2, f32[5,32,16,1]{3,2,1,0:T(8,128)S(1)} %copy.37, f32[5,32,16,128]{3,2,1,0:T(8,128)S(1)} %copy-done.1, ...), kind=kLoop, calls=%fused_computation.50 | loop fusion | flops 5242880 | bytes 4212640 | tf_op jit(solution)/shard_map/mul | solution.py:66
  52.3 0.7 fusion.40
  53.0 0.8 fusion.36
  53.8 0.8 fusion.32
  54.6 0.8 fusion.27
  55.3 0.7 broadcast_dynamic-update-slice_fusion.1
  56.1 2.6 %reduce = f32[64,2560]{1,0:T(8,128)S(1)} reduce(f32[64,1,2560]{2,1,0:T(1,128)} %all-to-all-done, f32[]{:T(128)} %constant.123), dimensions={1}, to_apply=%all_to_all.7.reduce_sub_computation | reduce | bytes 1310724 | tf_op jit(solution)/shard_map/all_to_all | solution.py:135
  58.9 1.5 fusion.3
  60.5 28.1 %psum.21 = f32[5,32,16]{2,1,0:T(8,128)S(1)} all-reduce(f32[5,32,16]{2,1,0:T(8,128)S(1)} %reshape.200), channel_id=1, replica_groups=mesh['stream'=8,'span'=16,'vert'=4] {'stream'}, use_global_device_ids=true, to_apply=%region_3.4 | all-reduce | flops 2560 | bytes 20480 | tf_op jit(solution)/shard_map/psum | solution.py:151
  88.6 7.5 %multiply_add_fusion = f32[5,32,16,128]{3,2,1,0:T(8,128)S(1)} fusion(f32[5,32,16,128]{3,2,1,0:T(8,128)S(1)} %copy-done.1, f32[5,32,16,128]{3,2,1,0:T(8,128)} %broadcast_dynamic-update-slice_fusion.1, f32[5,32,16]{2,1,0:T(8,128)S(1)} %broadcast_add_fusion.1, f32[128]{0:T(128)S(1)} %compare_select_fusion.1, f32[32,16,128]{2,1,0:T(8,128)} %get-tuple-element.87, ...), kind=kLoop, calls=%fused_computation.45 | loop fusion | flops 13434880 | bytes 5009844 | tf_op jit(solution)/shard_map/add | solution.py:162
  96.1 1.9 fusion.51
  98.1 1.9 copy.44
  100.0 3.6 %collective-permute-start.6 = (f32[5,32,16,1]{1,2,3,0:T(8,128)S(1)}, f32[5,32,16,1]{1,2,3,0:T(8,128)S(1)}, u32[]{:S(2)}, u32[]{:S(2)}) collective-permute-start(f32[5,32,16,1]{1,2,3,0:T(8,128)S(1)} %copy.44), channel_id=1, source_target_pairs={{64,0},{128,64},{192,128},{256,192},{320,256},{384,320},{448,384},... | collective-permute-start | bytes 30728 | tf_op jit(solution)/shard_map/ppermute | solution.py:34
  103.6 1.9 copy.46
  105.5 3.4 %collective-permute-start.7 = (f32[5,32,16,1]{1,2,3,0:T(8,128)S(1)}, f32[5,32,16,1]{1,2,3,0:T(8,128)S(1)}, u32[]{:S(2)}, u32[]{:S(2)}) collective-permute-start(f32[5,32,16,1]{1,2,3,0:T(8,128)S(1)} %copy.46), channel_id=1, source_target_pairs={{0,64},{64,128},{128,192},{192,256},{256,320},{320,384},{384,448},... | collective-permute-start | bytes 30728 | tf_op jit(solution)/shard_map/ppermute | solution.py:31
  109.0 1.6 copy.45
  110.6 0.7 collective-permute-done.7
  111.4 1.6 copy.47
  113.0 2.9 %pad_maximum_fusion.36 = (f32[5,32,1,130]{3,2,1,0:T(1,128)S(1)}, f32[5,32,1,130]{3,2,1,0:T(1,128)S(1)}) fusion(f32[5,32,16,1]{3,2,1,0:T(8,128)} %copy.45, f32[5,32,16,128]{3,2,1,0:T(8,128)S(1)} %multiply_add_fusion, f32[5,32,16,1]{3,2,1,0:T(8,128)} %copy.47), kind=kLoop, calls=%fused_computation.118 | loop fusion | flops 83200 | bytes 1497600 | tf_op jit(solution)/shard_map/concatenate | solution.py:35
  115.9 1.4 collective-permute-start.8
  117.3 3.3 %collective-permute-start.9 = (f32[5,32,1,130]{3,2,1,0:T(1,128)S(1)}, f32[5,32,1,130]{3,2,1,0:T(1,128)S(1)}, u32[]{:S(2)}, u32[]{:S(2)}) collective-permute-start(f32[5,32,1,130]{3,2,1,0:T(1,128)S(1)} %get-tuple-element.75), channel_id=1, source_target_pairs={{0,4},{4,8},{8,12},{12,16},{16,20},{20,24},{24,28},{28,32},{32,36}... | collective-permute-start | bytes 249608 | tf_op jit(solution)/shard_map/ppermute | solution.py:31
  120.7 0.7 collective-permute-done.9
  121.5 1.3 collective-permute-start.10
  122.8 5.1 %collective-permute-start.11 = (f32[5,1,18,130]{3,2,1,0:T(8,128)S(1)}, f32[5,1,18,130]{3,2,1,0:T(8,128)S(1)}, u32[]{:S(2)}, u32[]{:S(2)}) collective-permute-start(f32[5,1,18,130]{3,2,1,0:T(8,128)S(1)} %get-tuple-element.69), channel_id=1, source_target_pairs={{0,1},{1,2},{2,3},{4,5},{5,6},{6,7},{8,9},{9,10},{10,11},{12,13},{... | collective-permute-start | bytes 140408 | tf_op jit(solution)/shard_map/ppermute | solution.py:31
  127.9 1.1 broadcast_multiply_fusion.1
  129.0 1.3 collective-permute-done.11
  130.3 3.1 %broadcast_multiply_fusion = (f32[5,32,16,128]{3,2,1,0:T(8,128)S(1)}, f32[5,32,16,128]{3,2,1,0:T(8,128)S(1)}) fusion(f32[5,1,18,130]{3,2,1,0:T(8,128)S(1)} %collective-permute-done.10, f32[5,32,1,130]{3,2,1,0:T(1,128)S(1)} %collective-permute-done.8, f32[5,32,16,1]{3,2,1,0:T(8,128)S(1)} %copy-done.4, f32[5,32,16,128]{3,2,1,0:T(8,128)S(1)} %multiply_add_fusion, ...), kind=kLoop, calls=%fused_computation.47 | loop fusion | flops 5242880 | bytes 4212640 | tf_op jit(solution)/shard_map/mul | solution.py:66
  133.8 5.0 %add_multiply_fusion = f32[5,32,16,128]{3,2,1,0:T(8,128)S(1)} fusion(f32[5,32,16,128]{3,2,1,0:T(8,128)S(1)} %broadcast_dynamic-update-slice_fusion, f32[5,32,16,128]{3,2,1,0:T(8,128)S(1)} %multiply_add_fusion, f32[5,32,16,128]{3,2,1,0:T(8,128)S(1)} %copy-done.1, f32[32,16,128]{2,1,0:T(8,128)S(1)} %get-tuple-element.82, ...), kind=kLoop, calls=%fused_computation.44 | loop fusion | flops 14090240 | bytes 6320564 | tf_op jit(solution)/shard_map/mul | solution.py:164
  138.8 1.0 copy-done.7
  139.9 11.8 %gather_fusion = f32[2048]{0:T(1024)S(1)} fusion(f32[65536]{0:T(1024)S(1)} %bitcast.150, s32[2048]{0:T(1024)S(1)} %broadcast_clamp_fusion), kind=kCustom, calls=%fused_computation | custom fusion | bytes 24576 | tf_op jit(solution)/shard_map/gather | solution.py:166
  151.7 25.6 %all-gather = f32[32768]{0:T(1024)S(1)} all-gather(f32[2048]{0:T(1024)S(1)} %gather_fusion), channel_id=2, replica_groups=mesh['stream'=8,'span'=16,'vert'=4] {'span'}, dimensions={0}, use_global_device_ids=true | all-gather | bytes 139264 | tf_op jit(solution)/shard_map/all_gather | solution.py:168
  177.4 10.6 %while.11 = (s32[]{:T(128)}, f32[3,64]{1,0:T(4,128)S(1)}, f32[16,3,2048]{2,0,1:T(8,128)S(1)}, s32[16,2048]{1,0:T(8,128)S(1)}, s32[]{:T(128)}, /*index=5*/s32[]{:T(128)}) while((s32[]{:T(128)}, f32[3,64]{1,0:T(4,128)S(1)}, f32[16,3,2048]{2,0,1:T(8,128)S(1)}, s32[16,2048]{1,0:T(8,128)S(1)}, s32[]{:T(128)}, /*index=5*/s32[]{:T(128)}) %tuple.46), condition=%wide.region_5.6_spmd.clone, body=%wide.region_4.5_spmd.clone.sunk | while | flops 4850051 | bytes 99927 | solution.py:111
  177.5 0.6 convolution_add_fusion.2
  178.1 0.6 convolution_add_fusion.2
  178.8 0.6 convolution_add_fusion.2
  179.5 0.6 convolution_add_fusion.2
  180.1 0.6 convolution_add_fusion.2
  180.8 0.6 convolution_add_fusion.2
  181.5 0.6 convolution_add_fusion.2
  182.1 0.6 convolution_add_fusion.2
  182.8 0.6 convolution_add_fusion.2
  184.1 0.6 convolution_add_fusion.2
  187.4 0.6 convolution_add_fusion.2
  188.2 12.4 %psum.22 = f32[32]{0:T(128)S(1)} all-reduce(f32[32]{0:T(128)S(1)} %convolution_bitcast_fusion), channel_id=1, replica_groups=mesh['stream'=8,'span'=16,'vert'=4] {'vert'}, use_global_device_ids=true, to_apply=%region_6.7 | all-reduce | flops 32 | bytes 256 | tf_op jit(solution)/shard_map/psum | solution.py:22
  200.6 16.1 %psum.23 = f32[32]{0:T(128)} all-reduce(f32[32]{0:T(128)S(1)} %psum.22), channel_id=1, replica_groups=mesh['stream'=8,'span'=16,'vert'=4] {'stream'}, use_global_device_ids=true, to_apply=%region_7.8 | all-reduce | flops 32 | bytes 256 | tf_op jit(solution)/shard_map/psum | solution.py:22
  (113 shorter events, 6.0 us)
Async XLA Ops:
  0.6 187.4 %copy-start = (f32[3,64,32]{1,2,0:T(8,128)S(1)}, f32[3,64,32]{1,2,0:T(8,128)}, u32[]{:S(2)}) copy-start(f32[3,64,32]{1,2,0:T(8,128)} %param.20) | copy-start | bytes 73732
  2.8 8.3 %copy-start.14 = (s32[64,1]{0,1:T(1,128)S(1)}, s32[64,1]{0,1:T(1,128)}, u32[]{:S(2)}) copy-start(s32[64,1]{0,1:T(1,128)} %param.16) | copy-start | bytes 772
  2.8 8.7 %copy-start.11 = (f32[64,5,256]{2,0,1:T(8,128)S(1)}, f32[64,5,256]{2,0,1:T(8,128)}, u32[]{:S(2)}) copy-start(f32[64,5,256]{2,0,1:T(8,128)} %param.15) | copy-start | bytes 983044
  3.4 27.1 %collective-permute-start = (f32[5,32,16,1]{1,2,3,0:T(8,128)S(1)}, f32[5,32,16,1]{1,2,3,0:T(8,128)S(1)}, u32[]{:S(2)}, u32[]{:S(2)}) collective-permute-start(f32[5,32,16,1]{1,2,3,0:T(8,128)S(1)} %copy.55), channel_id=1, source_target_pairs={{64,0},{128,64},{192,128},{256,192},{320,256},{384,320},{448,384},... | collective-permute-start | bytes 30728 | tf_op jit(solution)/shard_map/ppermute | solution.py:34
  6.4 24.8 %collective-permute-start.1 = (f32[5,32,16,1]{1,2,3,0:T(8,128)S(1)}, f32[5,32,16,1]{1,2,3,0:T(8,128)S(1)}, u32[]{:S(2)}, u32[]{:S(2)}) collective-permute-start(f32[5,32,16,1]{1,2,3,0:T(8,128)S(1)} %copy.56), channel_id=1, source_target_pairs={{0,64},{64,128},{128,192},{192,256},{256,320},{320,384},{384,448},... | collective-permute-start | bytes 30728 | tf_op jit(solution)/shard_map/ppermute | solution.py:31
  11.9 15.7 %copy-start.1 = (f32[5,32,16,128]{3,2,1,0:T(8,128)S(1)}, f32[5,32,16,128]{3,2,1,0:T(8,128)}, u32[]{:S(2)}) copy-start(f32[5,32,16,128]{3,2,1,0:T(8,128)} %param.13) | copy-start | bytes 3932164
  13.5 15.1 %copy-start.13 = (s32[1,1,1,2048]{3,2,1,0:T(1,128)S(1)}, s32[1,1,1,2048]{3,2,1,0:T(1,128)}, u32[]{:S(2)}) copy-start(s32[1,1,1,2048]{3,2,1,0:T(1,128)} %param.17) | copy-start | bytes 24580
  13.5 42.6 %all-to-all-start = ((f32[64,1,2560]{2,1,0:T(1,128)}), f32[64,1,2560]{2,1,0:T(1,128)}, u32[]{:S(2)}, u32[]{:S(2)}) async-start(f32[64,1,2560]{2,1,0:T(1,128)} %all_to_all.8), calls=%async_computation | async-start | bytes 1310720 | tf_op jit(solution)/shard_map/all_to_all | solution.py:135
  31.2 17.9 %copy-start.2 = (f32[5,32,16,1]{3,2,1,0:T(8,128)}, f32[5,32,16,1]{3,2,1,0:T(8,128)S(1)}, u32[]{:S(2)}) copy-start(f32[5,32,16,1]{3,2,1,0:T(8,128)S(1)} %copy.37) | copy-start | bytes 30724
  32.8 7.8 %copy-start.3 = (f32[5,32,16,1]{3,2,1,0:T(8,128)S(1)}, f32[5,32,16,1]{3,2,1,0:T(8,128)}, u32[]{:S(2)}) copy-start(f32[5,32,16,1]{3,2,1,0:T(8,128)} %copy.39) | copy-start | bytes 30724
  35.3 4.4 %collective-permute-start.2 = (f32[5,32,1,130]{3,2,1,0:T(1,128)S(1)}, f32[5,32,1,130]{3,2,1,0:T(1,128)S(1)}, u32[]{:S(2)}, u32[]{:S(2)}) collective-permute-start(f32[5,32,1,130]{3,2,1,0:T(1,128)S(1)} %get-tuple-element.80), channel_id=1, source_target_pairs={{4,0},{8,4},{12,8},{16,12},{20,16},{24,20},{28,24},{32,28},{36,32}... | collective-permute-start | bytes 249608 | tf_op jit(solution)/shard_map/ppermute | solution.py:34
  36.6 4.0 %collective-permute-start.3 = (f32[5,32,1,130]{3,2,1,0:T(1,128)S(1)}, f32[5,32,1,130]{3,2,1,0:T(1,128)S(1)}, u32[]{:S(2)}, u32[]{:S(2)}) collective-permute-start(f32[5,32,1,130]{3,2,1,0:T(1,128)S(1)} %get-tuple-element.79), channel_id=1, source_target_pairs={{0,4},{4,8},{8,12},{12,16},{16,20},{20,24},{24,28},{28,32},{32,36}... | collective-permute-start | bytes 249608 | tf_op jit(solution)/shard_map/ppermute | solution.py:31
  40.8 7.2 %collective-permute-start.4 = (f32[5,1,18,130]{3,2,1,0:T(8,128)S(1)}, f32[5,1,18,130]{3,2,1,0:T(8,128)S(1)}, u32[]{:S(2)}, u32[]{:S(2)}) collective-permute-start(f32[5,1,18,130]{3,2,1,0:T(8,128)S(1)} %get-tuple-element.72), channel_id=1, source_target_pairs={{1,0},{2,1},{3,2},{5,4},{6,5},{7,6},{9,8},{10,9},{11,10},{13,12},{... | collective-permute-start | bytes 140408 | tf_op jit(solution)/shard_map/ppermute | solution.py:34
  42.1 7.0 %collective-permute-start.5 = (f32[5,1,18,130]{3,2,1,0:T(8,128)S(1)}, f32[5,1,18,130]{3,2,1,0:T(8,128)S(1)}, u32[]{:S(2)}, u32[]{:S(2)}) collective-permute-start(f32[5,1,18,130]{3,2,1,0:T(8,128)S(1)} %get-tuple-element.71), channel_id=1, source_target_pairs={{0,1},{1,2},{2,3},{4,5},{5,6},{6,7},{8,9},{9,10},{10,11},{12,13},{... | collective-permute-start | bytes 140408 | tf_op jit(solution)/shard_map/ppermute | solution.py:31
  48.0 4.3 %copy-start.6 = (f32[32,16,128]{2,1,0:T(8,128)S(1)}, f32[32,16,128]{2,1,0:T(8,128)}, u32[]{:S(2)}) copy-start(f32[32,16,128]{2,1,0:T(8,128)} %param.14) | copy-start | bytes 786436
  48.0 4.3 %copy-start.8 = (f32[5,1,18,130]{3,2,1,0:T(8,128)}, f32[5,1,18,130]{3,2,1,0:T(8,128)S(1)}, u32[]{:S(2)}) copy-start(f32[5,1,18,130]{3,2,1,0:T(8,128)S(1)} %collective-permute-done.4) | copy-start | bytes 140404
  49.1 3.2 %copy-start.9 = (f32[5,1,18,130]{3,2,1,0:T(8,128)}, f32[5,1,18,130]{3,2,1,0:T(8,128)S(1)}, u32[]{:S(2)}) copy-start(f32[5,1,18,130]{3,2,1,0:T(8,128)S(1)} %collective-permute-done.5) | copy-start | bytes 140404
  58.7 29.8 %copy-start.16 = (f32[5]{0:T(128)S(1)}, f32[5]{0:T(128)}, u32[]{:S(2)}) copy-start(f32[5]{0:T(128)} %constant.116.clone) | copy-start | bytes 64
  58.7 29.9 %copy-start.15 = (f32[5]{0:T(128)S(1)}, f32[5]{0:T(128)}, u32[]{:S(2)}) copy-start(f32[5]{0:T(128)} %constant.117.clone) | copy-start | bytes 64
  98.1 10.9 %copy-start.12 = (s32[1,16,1,2048]{3,2,1,0:T(1,128)S(1)}, s32[1,16,1,2048]{3,2,1,0:T(1,128)}, u32[]{:S(2)}) copy-start(s32[1,16,1,2048]{3,2,1,0:T(1,128)} %param.19) | copy-start | bytes 393220
  100.0 9.0 %collective-permute-start.6 = (f32[5,32,16,1]{1,2,3,0:T(8,128)S(1)}, f32[5,32,16,1]{1,2,3,0:T(8,128)S(1)}, u32[]{:S(2)}, u32[]{:S(2)}) collective-permute-start(f32[5,32,16,1]{1,2,3,0:T(8,128)S(1)} %copy.44), channel_id=1, source_target_pairs={{64,0},{128,64},{192,128},{256,192},{320,256},{384,320},{448,384},... | collective-permute-start | bytes 30728 | tf_op jit(solution)/shard_map/ppermute | solution.py:34
  105.5 5.9 %collective-permute-start.7 = (f32[5,32,16,1]{1,2,3,0:T(8,128)S(1)}, f32[5,32,16,1]{1,2,3,0:T(8,128)S(1)}, u32[]{:S(2)}, u32[]{:S(2)}) collective-permute-start(f32[5,32,16,1]{1,2,3,0:T(8,128)S(1)} %copy.46), channel_id=1, source_target_pairs={{0,64},{64,128},{128,192},{192,256},{256,320},{320,384},{384,448},... | collective-permute-start | bytes 30728 | tf_op jit(solution)/shard_map/ppermute | solution.py:31
  113.0 8.4 %copy-start.5 = (f32[5,32,16,1]{3,2,1,0:T(8,128)S(1)}, f32[5,32,16,1]{3,2,1,0:T(8,128)}, u32[]{:S(2)}) copy-start(f32[5,32,16,1]{3,2,1,0:T(8,128)} %copy.47) | copy-start | bytes 30724
  115.9 5.5 %copy-start.4 = (f32[5,32,16,1]{3,2,1,0:T(8,128)S(1)}, f32[5,32,16,1]{3,2,1,0:T(8,128)}, u32[]{:S(2)}) copy-start(f32[5,32,16,1]{3,2,1,0:T(8,128)} %copy.45) | copy-start | bytes 30724
  115.9 4.8 %collective-permute-start.8 = (f32[5,32,1,130]{3,2,1,0:T(1,128)S(1)}, f32[5,32,1,130]{3,2,1,0:T(1,128)S(1)}, u32[]{:S(2)}, u32[]{:S(2)}) collective-permute-start(f32[5,32,1,130]{3,2,1,0:T(1,128)S(1)} %get-tuple-element.76), channel_id=1, source_target_pairs={{4,0},{8,4},{12,8},{16,12},{20,16},{24,20},{28,24},{32,28},{36,32}... | collective-permute-start | bytes 249608 | tf_op jit(solution)/shard_map/ppermute | solution.py:34
  117.3 4.0 %collective-permute-start.9 = (f32[5,32,1,130]{3,2,1,0:T(1,128)S(1)}, f32[5,32,1,130]{3,2,1,0:T(1,128)S(1)}, u32[]{:S(2)}, u32[]{:S(2)}) collective-permute-start(f32[5,32,1,130]{3,2,1,0:T(1,128)S(1)} %get-tuple-element.75), channel_id=1, source_target_pairs={{0,4},{4,8},{8,12},{12,16},{16,20},{20,24},{24,28},{28,32},{32,36}... | collective-permute-start | bytes 249608 | tf_op jit(solution)/shard_map/ppermute | solution.py:31
  121.5 7.5 %collective-permute-start.10 = (f32[5,1,18,130]{3,2,1,0:T(8,128)S(1)}, f32[5,1,18,130]{3,2,1,0:T(8,128)S(1)}, u32[]{:S(2)}, u32[]{:S(2)}) collective-permute-start(f32[5,1,18,130]{3,2,1,0:T(8,128)S(1)} %get-tuple-element.70), channel_id=1, source_target_pairs={{1,0},{2,1},{3,2},{5,4},{6,5},{7,6},{9,8},{10,9},{11,10},{13,12},{... | collective-permute-start | bytes 140408 | tf_op jit(solution)/shard_map/ppermute | solution.py:34
  122.8 7.5 %collective-permute-start.11 = (f32[5,1,18,130]{3,2,1,0:T(8,128)S(1)}, f32[5,1,18,130]{3,2,1,0:T(8,128)S(1)}, u32[]{:S(2)}, u32[]{:S(2)}) collective-permute-start(f32[5,1,18,130]{3,2,1,0:T(8,128)S(1)} %get-tuple-element.69), channel_id=1, source_target_pairs={{0,1},{1,2},{2,3},{4,5},{5,6},{6,7},{8,9},{9,10},{10,11},{12,13},{... | collective-permute-start | bytes 140408 | tf_op jit(solution)/shard_map/ppermute | solution.py:31
  138.8 1.1 copy-start.7
  139.9 37.4 %copy-start.10 = (f32[1,16,1,3,2048]{4,2,3,1,0:T(1,128)S(1)}, f32[1,16,1,3,2048]{4,2,3,1,0:T(1,128)}, u32[]{:S(2)}) copy-start(f32[1,16,1,3,2048]{4,2,3,1,0:T(1,128)} %param.18) | copy-start | bytes 1179652
